TPU v7x, 256 devices: a whole 4x4x8 slice. The times are simulated.
256 devices in a mesh: freq: 16 (over z, core), bl: 16 (over y, x).
Axes of the slice: x: 4, y: 4, z: 8, core: 2. Of those that a mesh axis runs over, the one named last changes fastest.
Arguments:
- visibilities: float32 [2, 64, 4, 131072], P(None, 'freq', None, 'bl')
- sky_model: bfloat16 [2, 64, 8, 4, 131072], P(None, 'freq', None, None, 'bl')
- flag_mask: int32 [4, 131072], P(None, 'bl'), may hold values from 0 to 1
- first_station: int32 [131072], P('bl'), may hold values from 0 to 511
- second_station: int32 [131072], P('bl'), may hold values from 0 to 511, as said below
- gain_start: float32 [2, 64, 8, 512], P(None, 'freq')
- dual_start: float32 [2, 64, 8, 512], P(None, 'freq'), may hold values from -1.8 to 1.8
- consensus_start: float32 [3, 2, 8, 512], replicated, may hold values from -27.495455 to 27.495455
- penalty: float32 [8], replicated, may hold values from 0.3 to 3
Outputs:
- gain_final: float32 [2, 64, 8, 512], P(None, 'freq')
- dual_final: float32 [2, 64, 8, 512], P(None, 'freq')
- consensus_final: float32 [3, 2, 8, 512], replicated
Inputs may be any that keep to these rules, and one draw needn't show every extreme that they name: `second_station`: differs from first_station on every baseline.
All inputs are finite; a program needn't handle non-finite values.
Results may differ from a plain program's by a relative error of at most 0.0003.
Values sent between devices are 32-bit elements; how exact they have to be, the bound alone decides.
No kernel may reach another device: no remote copies, remote signals or barrier semaphores. Data moves between devices by JAX's collectives and lax.ppermute only.
A program may use at most 64 MiB of HBM per device.

v0:
```python
import math
import jax
import jax.numpy as jnp
from jax import lax
from jax.sharding import PartitionSpec as P

NPOLY = 3
NIT = 3
precise = lax.Precision.HIGHEST


def poly_basis(channel_count, degree):
    positions = jnp.arange(channel_count).astype(jnp.float32)
    spread = (2.0 * positions + 1.0) / channel_count - 1.0
    columns = []
    for exponent in range(degree):
        column = spread**exponent
        for earlier in columns:
            column = column - jnp.sum(column * earlier) * earlier
        column = column / jnp.sqrt(jnp.sum(column * column))
        columns.append(column)
    return jnp.stack(columns, axis=1)


def visibility_products(
    sky_real,
    sky_imag,
    vis_real,
    vis_imag,
    weights,
    first_real,
    first_imag,
    second_gain_real,
    second_imag,
):
    apparent_real = sky_real * second_gain_real + sky_imag * second_imag
    apparent_imag = sky_imag * second_gain_real - sky_real * second_imag
    predicted_real = first_real * apparent_real - first_imag * apparent_imag
    predicted_imag = first_real * apparent_imag + first_imag * apparent_real
    leftover_real = weights * (vis_real - jnp.sum(predicted_real, axis=-3))
    leftover_imag = weights * (vis_imag - jnp.sum(predicted_imag, axis=-3))
    target_real = jnp.expand_dims(leftover_real, -3) + weights * predicted_real
    target_imag = jnp.expand_dims(leftover_imag, -3) + weights * predicted_imag
    mirror_real = sky_real * first_real - sky_imag * first_imag
    mirror_imag = sky_real * first_imag + sky_imag * first_real
    first_terms = jnp.stack(
        [
            jnp.sum(apparent_real * target_real + apparent_imag * target_imag, axis=-2),
            jnp.sum(apparent_real * target_imag - apparent_imag * target_real, axis=-2),
            jnp.sum(
                weights * (apparent_real * apparent_real + apparent_imag * apparent_imag), axis=-2
            ),
        ]
    )
    second_terms = jnp.stack(
        [
            jnp.sum(mirror_real * target_real + mirror_imag * target_imag, axis=-2),
            jnp.sum(mirror_imag * target_real - mirror_real * target_imag, axis=-2),
            jnp.sum(weights * (mirror_real * mirror_real + mirror_imag * mirror_imag), axis=-2),
        ]
    )
    return (first_terms, second_terms)


def gain_update(gain_values, summed, target, dual_values, weight):
    denom = summed[2] + weight
    new_real = (summed[0] + weight * target[0] - dual_values[0]) / denom
    new_imag = (summed[1] + weight * target[1] - dual_values[1]) / denom
    return 0.5 * (gain_values + jnp.stack([new_real, new_imag]))


def per_device(
    visibilities,
    sky_model,
    flag_mask,
    first_station,
    second_station,
    gain_start,
    dual_start,
    consensus_start,
    penalty,
):
    local_channels = visibilities.shape[1]
    directions = gain_start.shape[2]
    stations = gain_start.shape[3]
    antenna_pairs = visibilities.shape[3]
    block_length = math.gcd(antenna_pairs, 1024)
    count_of_blocks = antenna_pairs // block_length
    channel_count = local_channels * lax.axis_size("freq")
    basis_rows = poly_basis(channel_count, NPOLY)
    local_rows = lax.dynamic_slice_in_dim(
        basis_rows, lax.axis_index("freq") * local_channels, local_channels, 0
    )
    weight = penalty[:, None]
    target = jnp.einsum("fn,nckp->cfkp", local_rows, consensus_start, precision=precise)
    flag_weight = flag_mask.astype(jnp.float32)
    station_iota = lax.broadcasted_iota(jnp.int32, (stations, block_length), 0)
    contract = (((1,), (1,)), ((), ()))
    rows_total = 3 * local_channels * directions
    gain_now = gain_start
    for iteration in range(NIT):
        gain_table = gain_now.reshape(2 * local_channels * directions, stations)

        def add_block(position, totals):
            block_start = position * block_length
            first_ids = lax.dynamic_slice_in_dim(first_station, block_start, block_length, 0)
            second_station_index = lax.dynamic_slice_in_dim(
                second_station, block_start, block_length, 0
            )
            first_hot = (station_iota == first_ids[None, :]).astype(jnp.float32)
            second_hot = (station_iota == second_station_index[None, :]).astype(jnp.float32)
            first_gain = jnp.dot(
                gain_table, first_hot, precision=precise, preferred_element_type=jnp.float32
            ).reshape(2, local_channels, directions, 1, block_length)
            second_gain = jnp.dot(
                gain_table, second_hot, precision=precise, preferred_element_type=jnp.float32
            ).reshape(2, local_channels, directions, 1, block_length)
            sky_block = lax.dynamic_slice_in_dim(sky_model, block_start, block_length, 4).astype(
                jnp.float32
            )
            vis_block = lax.dynamic_slice_in_dim(visibilities, block_start, block_length, 3)
            mask_block = lax.dynamic_slice_in_dim(flag_weight, block_start, block_length, 1)
            first_terms, second_terms = visibility_products(
                sky_block[0],
                sky_block[1],
                vis_block[0],
                vis_block[1],
                mask_block,
                first_gain[0],
                first_gain[1],
                second_gain[0],
                second_gain[1],
            )
            first_terms = first_terms.reshape(rows_total, block_length)
            second_terms = second_terms.reshape(rows_total, block_length)
            first_sums = lax.dot_general(
                first_terms,
                first_hot,
                contract,
                precision=precise,
                preferred_element_type=jnp.float32,
            )
            second_sums = lax.dot_general(
                second_terms,
                second_hot,
                contract,
                precision=precise,
                preferred_element_type=jnp.float32,
            )
            return totals + first_sums + second_sums

        totals = lax.fori_loop(
            0, count_of_blocks, add_block, jnp.zeros((rows_total, stations), jnp.float32)
        )
        partial_sums = totals.reshape(3, local_channels, directions, stations)
        summed_all = lax.psum(partial_sums, "bl")
        gain_now = gain_update(gain_now, summed_all, target, dual_start, weight)
    shifted = gain_now + dual_start / weight
    local_part = jnp.einsum("fn,cfkp->nckp", local_rows, shifted, precision=precise)
    consensus_final = lax.psum(local_part, "freq")
    fitted = jnp.einsum("fn,nckp->cfkp", local_rows, consensus_final, precision=precise)
    dual_final = dual_start + weight * (gain_now - fitted)
    return (gain_now, dual_final, consensus_final)


def solution(mesh):
    in_specs = (
        P(None, "freq", None, "bl"),
        P(None, "freq", None, None, "bl"),
        P(None, "bl"),
        P("bl"),
        P("bl"),
        P(None, "freq", None, None),
        P(None, "freq", None, None),
        P(),
        P(),
    )
    out_specs = (P(None, "freq", None, None), P(None, "freq", None, None), P())
    return jax.shard_map(
        per_device, mesh=mesh, in_specs=in_specs, out_specs=out_specs, check_vma=False
    )
```

profile of v0, /device:TPU:1, one launch (start us, length us, event | category | flops | bytes accessed | tf_op | source)
XLA Modules:
  0.0 750.2 jit_solution(8116796445936718820)
XLA Ops:
  8.2 106.4 %while.45 = (s32[]{:T(128)}, f32[96,512]{1,0:T(8,128)S(1)}, bf16[2,4,8,4,8192]{4,3,2,1,0:T(4,128)(2,1)}, s32[8192]{0:T(1024)}, f32[64,512]{1,0:T(8,128)}, /*inde...) while((s32[]{:T(128)}, f32[96,512]{1,0:T(8,128)S(1)}, ...), condition=%wide.region_9.10_spmd.clone.clone, body=%wide.region_0.9_spmd.clone.clone.sunk | while | flops 2023342080 | bytes 14123225 | solution.py:152
  16.2 2.8 add_reduce_fusion.9
  29.5 2.8 add_reduce_fusion.9
  42.8 2.8 add_reduce_fusion.9
  56.1 2.8 add_reduce_fusion.9
  69.4 2.8 add_reduce_fusion.9
  82.7 2.8 add_reduce_fusion.9
  96.0 2.8 add_reduce_fusion.9
  109.3 2.8 add_reduce_fusion.9
  123.5 88.3 %all-reduce.5.cloned.1.call-done = f32[3,4,8,512]{3,1,2,0:T(4,128)} async-done(((f32[3,4,8,512]{3,1,2,0:T(4,128)}), f32[3,4,8,512]{3,1,2,0:T(4,128)}) %all-reduce.5.cloned.1.call-update) | async-done | bytes 196624 | tf_op jit(solution)/shard_map/psum | solution.py:156
  214.6 106.4 %while.46 = (s32[]{:T(128)}, f32[96,512]{1,0:T(8,128)}, bf16[2,4,8,4,8192]{4,3,2,1,0:T(4,128)(2,1)}, s32[8192]{0:T(1024)S(1)}, f32[64,512]{1,0:T(8,128)}, /*inde...) while((s32[]{:T(128)}, f32[96,512]{1,0:T(8,128)}, ...), condition=%wide.region_25.26_spmd.clone.clone, body=%wide.region_16.25_spmd.clone.clone.sunk | while | flops 2023342080 | bytes 15696145 | solution.py:152
  221.9 2.8 add_reduce_fusion.10
  235.2 2.8 add_reduce_fusion.10
  248.5 2.8 add_reduce_fusion.10
  288.3 2.8 add_reduce_fusion.10
  314.9 2.8 add_reduce_fusion.10
  323.0 93.6 %all-reduce.7.cloned.1.call-done = f32[3,4,8,512]{3,1,2,0:T(4,128)} async-done(((f32[3,4,8,512]{3,1,2,0:T(4,128)}), f32[3,4,8,512]{3,1,2,0:T(4,128)}) %all-reduce.7.cloned.1.call-update) | async-done | bytes 196624 | tf_op jit(solution)/shard_map/psum | solution.py:156
  418.5 111.6 %while.47 = (s32[]{:T(128)}, f32[96,512]{1,0:T(8,128)}, bf16[2,4,8,4,8192]{4,3,2,1,0:T(4,128)(2,1)}, s32[8192]{0:T(1024)S(1)}, f32[64,512]{1,0:T(8,128)}, /*inde...) while((s32[]{:T(128)}, f32[96,512]{1,0:T(8,128)}, ...), condition=%wide.region_36.37_spmd.clone.clone, body=%wide.region_27.36_spmd.clone.clone.sunk | while | flops 2023342080 | bytes 15761793 | solution.py:152
  426.4 2.8 add_reduce_fusion.11
  496.1 2.8 add_reduce_fusion.11
  510.1 2.8 add_reduce_fusion.11
  524.0 2.8 add_reduce_fusion.11
  531.9 93.8 %all-reduce.9.cloned.1.call-done = f32[3,4,8,512]{3,1,2,0:T(4,128)} async-done(((f32[3,4,8,512]{3,1,2,0:T(4,128)}), f32[3,4,8,512]{3,1,2,0:T(4,128)}) %all-reduce.9.cloned.1.call-update) | async-done | bytes 196624 | tf_op jit(solution)/shard_map/psum | solution.py:156
  629.4 110.6 %all-reduce.11.cloned.1.call-done = f32[3,2,8,512]{3,0,2,1:T(4,128)} async-done(((f32[3,2,8,512]{3,0,2,1:T(4,128)}), f32[3,2,8,512]{3,0,2,1:T(4,128)}) %all-reduce.11.cloned.1.call-update) | async-done | bytes 98320 | tf_op jit(solution)/shard_map/psum | solution.py:160
  (501 shorter events, 295.9 us)
Async XLA Ops:
  7.2 115.8 %copy-start = (f32[3,2,8,512]{3,2,1,0:T(8,128)S(1)}, f32[3,2,8,512]{3,2,1,0:T(8,128)}, u32[]{:S(2)}) copy-start(f32[3,2,8,512]{3,2,1,0:T(8,128)} %param.22) | copy-start | bytes 294916
  7.2 204.6 %all-reduce.5.cloned.1.call-start = ((), (), s32[]{:S(2)}) async-start(), calls=%async_computation | async-start | bytes 393216 | tf_op jit(solution)/shard_map/psum | solution.py:156
  8.2 114.6 %copy-start.2 = (f32[2,4,8,512]{3,2,1,0:T(8,128)S(1)}, f32[2,4,8,512]{3,2,1,0:T(8,128)}, u32[]{:S(2)}) copy-start(f32[2,4,8,512]{3,2,1,0:T(8,128)} %param.21) | copy-start | bytes 393220
  8.2 203.7 %copy-start.14 = (f32[8]{0:T(128)S(1)}, f32[8]{0:T(128)}, u32[]{:S(2)}) copy-start(f32[8]{0:T(128)} %param.23) | copy-start | bytes 100
  114.6 100.0 %copy-start.7 = (s32[8192]{0:T(1024)S(1)}, s32[8192]{0:T(1024)}, u32[]{:S(2)}) copy-start(s32[8192]{0:T(1024)} %get-tuple-element.1150) | copy-start | bytes 98308
  115.5 301.2 %all-reduce.7.cloned.1.call-start = ((), (), s32[]{:S(2)}) async-start(), calls=%async_computation.1 | async-start | bytes 393216 | tf_op jit(solution)/shard_map/psum | solution.py:156
  214.6 203.1 %copy-start.1 = (f32[64,512]{1,0:T(8,128)S(1)}, f32[64,512]{1,0:T(8,128)}, u32[]{:S(2)}) copy-start(f32[64,512]{1,0:T(8,128)} %get-tuple-element.1135) | copy-start | bytes 393220
  221.9 4.1 copy-start.3
  235.2 4.1 copy-start.3
  261.7 4.1 copy-start.3
  288.3 4.1 copy-start.3
  314.9 4.1 copy-start.3
  322.7 303.0 %all-reduce.9.cloned.1.call-start = ((), (), s32[]{:S(2)}) async-start(), calls=%async_computation.2 | async-start | bytes 393216 | tf_op jit(solution)/shard_map/psum | solution.py:156
  426.4 4.2 copy-start.9
  440.3 4.2 copy-start.9
  454.3 4.2 copy-start.9
  468.2 4.2 copy-start.9
  482.2 4.2 copy-start.9
  496.1 4.2 copy-start.9
  510.0 4.2 copy-start.9
  524.0 4.2 copy-start.9
  530.1 210.0 %copy-start.13 = (f32[64,3]{0,1:T(4,128)S(1)}, f32[64,3]{0,1:T(4,128)}, u32[]{:S(2)}) copy-start(f32[64,3]{0,1:T(4,128)} %copy-done.12) | copy-start | bytes 2308
  530.1 210.0 %copy-start.15 = (f32[8]{0:T(128)S(1)}, f32[8]{0:T(128)}, u32[]{:S(2)}) copy-start(f32[8]{0:T(128)} %param.23) | copy-start | bytes 100
  531.8 208.2 %all-reduce.11.cloned.1.call-start = ((), (), s32[]{:S(2)}) async-start(), calls=%async_computation.3 | async-start | bytes 262144 | tf_op jit(solution)/shard_map/psum | solution.py:160
  (52 other events, 77.0 us)
Sparse Core Ops, SparseCore 0:
  115.6 96.2 all-reduce.4
  322.8 93.7 all-reduce.6
  532.0 93.7 all-reduce.8
  628.9 111.1 all-reduce.10
where the time goes:
time: 755 us; the launch traced here: 750 us
  waiting for transfers between devices  386 us (51%)
  other arithmetic  148 us (20%)
  matrix products  147 us (19%)
  local copies, waits for them, and re-layouts  47.9 us (6%)
  between operations  16.6 us (2%)
    psum x3, waiting for transfers between devices, per_device(): summed_all = lax.psum(partial_sums, 'bl')  276 us
    psum x1, waiting for transfers between devices, per_device(): consensus_final = lax.psum(local_part, 'freq')  111 us
    reduce_sum x24, other arithmetic, visibility_products(): jnp.sum(mirror_real * target_real + mirror_imag * target_imag, axis=-2)  67.9 us
    dot_general x24, matrix products, add_block(): jnp.dot(gain_table, second_hot, precision=precise, preferred_element_type...  42.6 us
    dot_general x24, matrix products, add_block(): jnp.dot(gain_table, first_hot, precision=precise, preferred_element_type=...  42.6 us
    dot_general x24, matrix products, add_block(): lax.dot_general(first_terms, first_hot, contract, precision=precise, pref...  29.2 us
    dot_general x24, matrix products, add_block(): lax.dot_general(second_terms, second_hot, contract, precision=precise, pr...  28.8 us
    convert_element_type x24, other arithmetic, add_block(): lax.dynamic_slice_in_dim(sky_model, block_start, block_length, 4)  28.2 us
  transfers between devices with their start and end apart: 4, of which 4 were waited for; matrix products, arithmetic and copies ran while one was open for 1% of the time, Pallas kernels for 0%

commit v1 on v0

--- a/solution.py
+++ b/solution.py
@@ -157,7 +157,7 @@
         gain_now = gain_update(gain_now, summed_all, target, dual_start, weight)
     shifted = gain_now + dual_start / weight
     local_part = jnp.einsum("fn,cfkp->nckp", local_rows, shifted, precision=precise)
-    consensus_final = lax.psum(local_part, "freq")
+    consensus_final = jnp.sum(lax.all_gather(local_part, "freq"), axis=0)
     fitted = jnp.einsum("fn,nckp->cfkp", local_rows, consensus_final, precision=precise)
     dual_final = dual_start + weight * (gain_now - fitted)
     return (gain_now, dual_final, consensus_final)

time: 755 us -> 683 us (0.905)
  waiting for transfers between devices: 386 us -> 316 us
    psum x1 -> x0, waiting for transfers between devices: 111 us -> none  [per_device(): consensus_final = lax.psum(local_part, 'freq')]
    all_gather x0 -> x1, waiting for transfers between devices: none -> 40.1 us  [per_device(): consensus_final = jnp.sum(lax.all_gather(local_part, 'freq'), axis=0)]
where the time goes in v1:
time: 683 us; the launch traced here: 679 us
  waiting for transfers between devices  316 us (46%)
  other arithmetic  150 us (22%)
  matrix products  145 us (21%)
  local copies, waits for them, and re-layouts  46.9 us (7%)
  between operations  16.6 us (2%)
    psum x3, waiting for transfers between devices, per_device(): summed_all = lax.psum(partial_sums, 'bl')  276 us
    reduce_sum x24, other arithmetic, visibility_products(): jnp.sum(mirror_real * target_real + mirror_imag * target_imag, axis=-2)  67.6 us
    dot_general x24, matrix products, add_block(): jnp.dot(gain_table, first_hot, precision=precise, preferred_element_type=...  42.6 us
    dot_general x24, matrix products, add_block(): jnp.dot(gain_table, second_hot, precision=precise, preferred_element_type...  42.6 us
    all_gather x1, waiting for transfers between devices, per_device(): consensus_final = jnp.sum(lax.all_gather(local_part, 'freq'), axis=0)  40.1 us
    dot_general x24, matrix products, add_block(): lax.dot_general(first_terms, first_hot, contract, precision=precise, pref...  29.2 us
    dot_general x24, matrix products, add_block(): lax.dot_general(second_terms, second_hot, contract, precision=precise, pr...  28.8 us
    convert_element_type x24, other arithmetic, add_block(): lax.dynamic_slice_in_dim(sky_model, block_start, block_length, 4)  28.2 us
  transfers between devices with their start and end apart: 4, of which 4 were waited for; matrix products, arithmetic and copies ran while one was open for 1% of the time, Pallas kernels for 0%

profile of v1, /device:TPU:1, one launch (start us, length us, event | category | flops | bytes accessed | tf_op | source)
XLA Modules:
  0.0 678.6 jit_solution(7625958357424246029)
XLA Ops:
  8.2 106.3 %while.45 = (s32[]{:T(128)}, f32[96,512]{1,0:T(8,128)S(1)}, bf16[2,4,8,4,8192]{4,3,2,1,0:T(4,128)(2,1)}, s32[8192]{0:T(1024)}, f32[64,512]{1,0:T(8,128)}, /*inde...) while((s32[]{:T(128)}, f32[96,512]{1,0:T(8,128)S(1)}, ...), condition=%wide.region_9.10_spmd.clone.clone, body=%wide.region_0.9_spmd.clone.clone.sunk | while | flops 2023342080 | bytes 14123225 | solution.py:152
  16.2 2.8 add_reduce_fusion.9
  123.3 88.3 %all-reduce.4.cloned.1.call-done = f32[3,4,8,512]{3,1,2,0:T(4,128)} async-done(((f32[3,4,8,512]{3,1,2,0:T(4,128)}), f32[3,4,8,512]{3,1,2,0:T(4,128)}) %all-reduce.4.cloned.1.call-update) | async-done | bytes 196624 | tf_op jit(solution)/shard_map/psum | solution.py:156
  214.4 106.4 %while.46 = (s32[]{:T(128)}, f32[96,512]{1,0:T(8,128)}, bf16[2,4,8,4,8192]{4,3,2,1,0:T(4,128)(2,1)}, s32[8192]{0:T(1024)S(1)}, f32[64,512]{1,0:T(8,128)}, /*inde...) while((s32[]{:T(128)}, f32[96,512]{1,0:T(8,128)}, ...), condition=%wide.region_25.26_spmd.clone.clone, body=%wide.region_16.25_spmd.clone.clone.sunk | while | flops 2023342080 | bytes 15696145 | solution.py:152
  221.7 2.8 add_reduce_fusion.10
  235.0 2.8 add_reduce_fusion.10
  248.3 2.8 add_reduce_fusion.10
  261.6 2.8 add_reduce_fusion.10
  274.9 2.8 add_reduce_fusion.10
  288.2 2.8 add_reduce_fusion.10
  301.5 2.8 add_reduce_fusion.10
  314.8 2.8 add_reduce_fusion.10
  322.8 93.6 %all-reduce.6.cloned.1.call-done = f32[3,4,8,512]{3,1,2,0:T(4,128)} async-done(((f32[3,4,8,512]{3,1,2,0:T(4,128)}), f32[3,4,8,512]{3,1,2,0:T(4,128)}) %all-reduce.6.cloned.1.call-update) | async-done | bytes 196624 | tf_op jit(solution)/shard_map/psum | solution.py:156
  418.3 111.6 %while.47 = (s32[]{:T(128)}, f32[96,512]{1,0:T(8,128)}, bf16[2,4,8,4,8192]{4,3,2,1,0:T(4,128)(2,1)}, s32[8192]{0:T(1024)S(1)}, f32[64,512]{1,0:T(8,128)}, /*inde...) while((s32[]{:T(128)}, f32[96,512]{1,0:T(8,128)}, ...), condition=%wide.region_36.37_spmd.clone.clone, body=%wide.region_27.36_spmd.clone.clone.sunk | while | flops 2023342080 | bytes 15761793 | solution.py:152
  426.2 2.8 add_reduce_fusion.11
  440.1 2.8 add_reduce_fusion.11
  454.1 2.8 add_reduce_fusion.11
  468.0 2.8 add_reduce_fusion.11
  482.0 2.8 add_reduce_fusion.11
  495.9 2.8 add_reduce_fusion.11
  509.8 2.8 add_reduce_fusion.11
  523.8 2.8 add_reduce_fusion.11
  531.7 93.8 %all-reduce.8.cloned.1.call-done = f32[3,4,8,512]{3,1,2,0:T(4,128)} async-done(((f32[3,4,8,512]{3,1,2,0:T(4,128)}), f32[3,4,8,512]{3,1,2,0:T(4,128)}) %all-reduce.8.cloned.1.call-update) | async-done | bytes 196624 | tf_op jit(solution)/shard_map/psum | solution.py:156
  629.2 40.1 %all-gather.3.cloned.1.call-done = f32[48,2,8,512]{3,2,1,0:T(8,128)} async-done(((f32[3,2,8,512]{3,2,1,0:T(8,128)}), f32[48,2,8,512]{3,2,1,0:T(8,128)}) %all-gather.3.cloned.1.call-update) | async-done | bytes 1572880 | tf_op jit(solution)/shard_map/all_gather | solution.py:160
  (504 shorter events, 294.9 us)
Async XLA Ops:
  7.2 115.6 %copy-start = (f32[3,2,8,512]{3,2,1,0:T(8,128)S(1)}, f32[3,2,8,512]{3,2,1,0:T(8,128)}, u32[]{:S(2)}) copy-start(f32[3,2,8,512]{3,2,1,0:T(8,128)} %param.22) | copy-start | bytes 294916
  7.2 204.5 %all-reduce.4.cloned.1.call-start = ((), (), s32[]{:S(2)}) async-start(), calls=%async_computation | async-start | bytes 393216 | tf_op jit(solution)/shard_map/psum | solution.py:156
  8.2 114.4 %copy-start.3 = (f32[2,4,8,512]{3,2,1,0:T(8,128)S(1)}, f32[2,4,8,512]{3,2,1,0:T(8,128)}, u32[]{:S(2)}) copy-start(f32[2,4,8,512]{3,2,1,0:T(8,128)} %param.21) | copy-start | bytes 393220
  8.2 203.5 %copy-start.15 = (f32[8]{0:T(128)S(1)}, f32[8]{0:T(128)}, u32[]{:S(2)}) copy-start(f32[8]{0:T(128)} %param.23) | copy-start | bytes 100
  114.5 100.0 %copy-start.8 = (s32[8192]{0:T(1024)S(1)}, s32[8192]{0:T(1024)}, u32[]{:S(2)}) copy-start(s32[8192]{0:T(1024)} %get-tuple-element.1150) | copy-start | bytes 98308
  115.3 301.1 %all-reduce.6.cloned.1.call-start = ((), (), s32[]{:S(2)}) async-start(), calls=%async_computation.1 | async-start | bytes 393216 | tf_op jit(solution)/shard_map/psum | solution.py:156
  214.4 203.0 %copy-start.1 = (f32[64,512]{1,0:T(8,128)S(1)}, f32[64,512]{1,0:T(8,128)}, u32[]{:S(2)}) copy-start(f32[64,512]{1,0:T(8,128)} %get-tuple-element.1136) | copy-start | bytes 393220
  221.7 4.1 copy-start.4
  235.0 4.1 copy-start.4
  261.6 4.1 copy-start.4
  288.2 4.1 copy-start.4
  314.8 4.1 copy-start.4
  322.6 302.9 %all-reduce.8.cloned.1.call-start = ((), (), s32[]{:S(2)}) async-start(), calls=%async_computation.2 | async-start | bytes 393216 | tf_op jit(solution)/shard_map/psum | solution.py:156
  426.2 4.2 copy-start.10
  440.1 4.2 copy-start.10
  454.1 4.2 copy-start.10
  468.0 4.2 copy-start.10
  481.9 4.2 copy-start.10
  495.9 4.2 copy-start.10
  509.8 4.2 copy-start.10
  523.8 4.2 copy-start.10
  531.6 137.7 %all-gather.3.cloned.1.call-start = ((), (), s32[]{:S(2)}) async-start(), calls=%async_computation.3 | async-start | bytes 1671168 | tf_op jit(solution)/shard_map/all_gather | solution.py:160
  626.5 44.4 %copy-start.14 = (f32[64,3]{0,1:T(4,128)S(1)}, f32[64,3]{0,1:T(4,128)}, u32[]{:S(2)}) copy-start(f32[64,3]{0,1:T(4,128)} %copy-done.13) | copy-start | bytes 2308
  626.5 44.4 %copy-start.16 = (f32[8]{0:T(128)S(1)}, f32[8]{0:T(128)}, u32[]{:S(2)}) copy-start(f32[8]{0:T(128)} %param.23) | copy-start | bytes 100
  (53 other events, 78.2 us)
Sparse Core Ops, SparseCore 0:
  115.4 96.2 all-reduce.3
  322.7 93.6 all-reduce.5
  531.7 93.6 all-reduce.7
  628.6 40.6 all-gather.2
